TPU v7x, 256 devices: a 2x2x32 block of a 4x8x32 slice. The times are simulated.
256 devices in a mesh: member: 4 (over y, x), ty: 64 (over z, core).
Axes of the slice: x: 2, y: 2, z: 32, core: 2. Of those that a mesh axis runs over, the one named last changes fastest.
The devices are a block of a 4x8x32 slice.
Arguments:
- fields: float32 [64, 768, 6, 768], P('member', 'ty'), parts along dimension 0, may hold values from -6 to 6
- damp_four: float32 [64], P('member'), parts along dimension 0, may hold values from 0.004 to 0.03
- damp_six: float32 [64], P('member'), parts along dimension 0, may hold values from 0.0008 to 0.006
- metric: float32 [4, 768, 6, 768], P(None, 'ty'), may hold values from 0.1 to 1.9
- seam_table: int32 [6, 4, 3], replicated, may hold values from 0 to 5
Outputs:
- damped: float32 [64, 768, 6, 768], P('member', 'ty'), parts along dimension 0
There are 4 independent parts, one for each index of `member`. A program takes and returns all parts, laid end to end along the dimension named above; an argument that names none is the same for every part. Nothing has to cross between parts.
Inputs may be any that keep to these rules, and one draw needn't show every extreme that they name: The table describes the surface of a cube with every face seen from outside: the joining is symmetric, no face is joined to itself, and r is 1 exactly when both edges are among (south, east) or both among (north, west).
All inputs are finite; a program needn't handle non-finite values.
Results may differ from a plain program's by a relative error of at most 0.00005.
Values sent between devices are 32-bit elements; how exact they have to be, the bound alone decides.
A program may use at most 64 MiB of HBM per device.

v0:
```python
import jax
import jax.numpy as jnp
from jax import lax
from jax.sharding import PartitionSpec as P


def with_halo(cells, sides, width):
    for axis, dim in sides:
        count = lax.axis_size(axis)
        ends = count - 1
        head = lax.slice_in_dim(cells, 0, width, axis=dim)
        tail = lax.slice_in_dim(cells, cells.shape[dim] - width, cells.shape[dim], axis=dim)
        cells = jnp.concatenate(
            [
                lax.ppermute(tail, axis, [(i, (i + 1) % count) for i in range(ends)]),
                cells,
                lax.ppermute(head, axis, [((i + 1) % count, i) for i in range(ends)]),
            ],
            axis=dim,
        )
    return cells


def strip_edges(source):
    east_cells = jnp.transpose(source[:, :, :, -1], (0, 2, 1))
    west_cells = jnp.transpose(source[:, :, :, 0], (0, 2, 1))
    return jnp.stack([east_cells, west_cells], axis=2)


def gather_edges(source):
    tile_index = lax.axis_index("ty")
    tile_count = lax.axis_size("ty")
    strip_rows = source.shape[1]
    row_width = source.shape[3]
    strip_cells = strip_edges(source)
    first_row = jnp.where(tile_index == 0, source[:, 0], 0.0)
    last_row = jnp.where(tile_index == tile_count - 1, source[:, -1], 0.0)
    blank = jnp.zeros(strip_cells.shape[:3] + (row_width,), jnp.float32)
    placed = lax.dynamic_update_slice_in_dim(blank, strip_cells, tile_index * strip_rows, 3)
    rim_cells = jnp.stack([first_row, placed[:, :, 0], last_row, placed[:, :, 1]], axis=2)
    edge_set = lax.psum(rim_cells, "ty")
    return edge_set


def seam_halo(edge_set, seam_table):
    levels = edge_set.shape[0]
    row_width = edge_set.shape[3]
    flattened = edge_set.reshape(levels, 24, row_width)
    picked = (seam_table[:, :, 0] * 4 + seam_table[:, :, 1]).reshape(24)
    onehot = (picked[:, None] == jnp.arange(24, dtype=jnp.int32)[None, :]).astype(jnp.float32)
    neighbor = jnp.einsum("jk,lkc->ljc", onehot, flattened, precision=lax.Precision.HIGHEST)
    neighbor = neighbor.reshape(levels, 6, 4, row_width)
    flipped = (seam_table[:, :, 2] == 1)[None, :, :, None]
    return jnp.where(flipped, neighbor[..., ::-1], neighbor)


def laplace(source, metric, seam_table):
    tile_index = lax.axis_index("ty")
    tile_count = lax.axis_size("ty")
    strip_rows = source.shape[1]
    padded = with_halo(source, (("ty", 1),), 1)
    halo_cells = seam_halo(gather_edges(source), seam_table)
    south_row = jnp.where(tile_index == 0, halo_cells[:, :, 0], padded[:, 0])
    north_row = jnp.where(tile_index == tile_count - 1, halo_cells[:, :, 2], padded[:, -1])
    row_start = tile_index * strip_rows
    west_cells = jnp.transpose(
        lax.dynamic_slice_in_dim(halo_cells[:, :, 3], row_start, strip_rows, 2), (0, 2, 1)
    )[..., None]
    east_cells = jnp.transpose(
        lax.dynamic_slice_in_dim(halo_cells[:, :, 1], row_start, strip_rows, 2), (0, 2, 1)
    )[..., None]
    padded_x = jnp.concatenate([west_cells, source, east_cells], axis=3)
    padded_y = jnp.concatenate([south_row[:, None], source, north_row[:, None]], axis=1)
    return (
        metric[0] * (padded_x[..., :-2] - source)
        + metric[1] * (padded_x[..., 2:] - source)
        + metric[2] * (padded_y[:, :-2] - source)
        + metric[3] * (padded_y[:, 2:] - source)
    )


def per_device(fields, damp_four, damp_six, metric, seam_table):
    second = laplace(fields, metric, seam_table)
    fourth = laplace(second, metric, seam_table)
    sixth = laplace(fourth, metric, seam_table)
    return fields - damp_four[:, None, None, None] * fourth + damp_six[:, None, None, None] * sixth


def solution(mesh):
    placed = (
        P("member", "ty", None, None),
        P("member"),
        P("member"),
        P(None, "ty", None, None),
        P(),
    )
    return jax.shard_map(
        per_device,
        mesh=mesh,
        in_specs=placed,
        out_specs=P("member", "ty", None, None),
        check_vma=False,
    )
```

profile of v0, /device:TPU:38, one launch (start us, length us, event | category | flops | bytes accessed | tf_op | source)
XLA Modules:
  0.0 1358.7 jit_solution(17897617132193836712)
XLA Ops:
  6.6 2.6 fusion.54
  23.6 2.6 reshape.130
  26.4 4.2 collective-permute-start
  32.2 3.4 fusion.58
  38.7 397.7 %all-reduce.4.cloned.1.call-done = f32[16,24,768]{2,1,0:T(8,128)} async-done(((f32[16,24,768]{2,1,0:T(8,128)}), f32[16,24,768]{2,1,0:T(8,128)}) %all-reduce.4.cloned.1.call-update) | async-done | bytes 1179664 | tf_op jit(solution)/shard_map/psum | solution.py:41
  439.7 4.7 rev.9
  456.3 4.7 fusion.26
  477.0 2.6 reshape.132
  479.7 4.6 collective-permute-start.2
  485.8 386.8 %all-reduce.6.cloned.1.call-done = f32[16,24,768]{2,1,0:T(8,128)} async-done(((f32[16,24,768]{2,1,0:T(8,128)}), f32[16,24,768]{2,1,0:T(8,128)}) %all-reduce.6.cloned.1.call-update) | async-done | bytes 1179664 | tf_op jit(solution)/shard_map/psum | solution.py:41
  872.6 3.0 convolution_bitcast_fusion.1
  875.6 2.6 reshape.133
  878.1 2.7 copy.98
  880.8 4.7 rev.10
  894.0 2.4 copy.101
  897.7 9.4 fusion.15
  923.1 2.6 reshape.134
  925.8 4.6 collective-permute-start.4
  931.9 386.8 %all-reduce.8.cloned.1.call-done = f32[16,24,768]{2,1,0:T(8,128)} async-done(((f32[16,24,768]{2,1,0:T(8,128)}), f32[16,24,768]{2,1,0:T(8,128)}) %all-reduce.8.cloned.1.call-update) | async-done | bytes 1179664 | tf_op jit(solution)/shard_map/psum | solution.py:41
  1318.7 3.0 convolution_bitcast_fusion
  1321.7 2.6 reshape.135
  1324.3 2.7 copy.105
  1326.9 4.7 rev.11
  1341.5 10.6 fusion.4
  (92 shorter events, 89.1 us)
Async XLA Ops:
  6.5 13.2 copy-start
  6.5 429.8 %all-reduce.4.cloned.1.call-start = ((), (), s32[]{:S(2)}) async-start(), calls=%async_computation | async-start | bytes 2359296 | tf_op jit(solution)/shard_map/psum | solution.py:41
  21.9 10.1 copy-start.6
  26.3 846.2 %all-reduce.6.cloned.1.call-start = ((), (), s32[]{:S(2)}) async-start(), calls=%async_computation.1 | async-start | bytes 2359296 | tf_op jit(solution)/shard_map/psum | solution.py:41
  26.4 428.7 %collective-permute-start = (f32[16,1,6,768]{3,0,2,1:T(8,128)}, f32[16,1,6,768]{3,0,2,1:T(8,128)}, u32[]{:S(2)}, u32[]{:S(2)}) collective-permute-start(f32[16,1,6,768]{3,0,2,1:T(8,128)} %get-tuple-element.17), channel_id=1, source_target_pairs={{0,1},{1,2},{2,3},{3,4},{4,5},{5,6},{6,7},{7,8},{8,9},{9,10},{10,1... | collective-permute-start | bytes 884744 | tf_op jit(solution)/shard_map/ppermute | solution.py:15
  30.6 424.5 %collective-permute-start.1 = (f32[16,1,6,768]{3,0,2,1:T(8,128)}, f32[16,1,6,768]{3,0,2,1:T(8,128)}, u32[]{:S(2)}, u32[]{:S(2)}) collective-permute-start(f32[16,1,6,768]{3,0,2,1:T(8,128)} %get-tuple-element.20), channel_id=1, source_target_pairs={{1,0},{2,1},{3,2},{4,3},{5,4},{6,5},{7,6},{8,7},{9,8},{10,9},{11,1... | collective-permute-start | bytes 884744 | tf_op jit(solution)/shard_map/ppermute | solution.py:17
  446.2 1.0 copy-start.4
  461.0 2.2 copy-start.2
  479.7 839.1 %all-reduce.8.cloned.1.call-start = ((), (), s32[]{:S(2)}) async-start(), calls=%async_computation.2 | async-start | bytes 2359296 | tf_op jit(solution)/shard_map/psum | solution.py:41
  479.7 416.7 %collective-permute-start.2 = (f32[16,1,6,768]{3,0,2,1:T(8,128)}, f32[16,1,6,768]{3,0,2,1:T(8,128)}, u32[]{:S(2)}, u32[]{:S(2)}) collective-permute-start(f32[16,1,6,768]{3,0,2,1:T(8,128)} %get-tuple-element.11), channel_id=1, source_target_pairs={{0,1},{1,2},{2,3},{3,4},{4,5},{5,6},{6,7},{7,8},{8,9},{9,10},{10,1... | collective-permute-start | bytes 884744 | tf_op jit(solution)/shard_map/ppermute | solution.py:15
  484.3 412.2 %collective-permute-start.3 = (f32[16,1,6,768]{3,0,2,1:T(8,128)}, f32[16,1,6,768]{3,0,2,1:T(8,128)}, u32[]{:S(2)}, u32[]{:S(2)}) collective-permute-start(f32[16,1,6,768]{3,0,2,1:T(8,128)} %get-tuple-element.14), channel_id=1, source_target_pairs={{1,0},{2,1},{3,2},{4,3},{5,4},{6,5},{7,6},{8,7},{9,8},{10,9},{11,1... | collective-permute-start | bytes 884744 | tf_op jit(solution)/shard_map/ppermute | solution.py:17
  887.5 1.0 copy-start.5
  907.1 2.2 copy-start.1
  925.8 414.5 %collective-permute-start.4 = (f32[16,1,6,768]{3,0,2,1:T(8,128)}, f32[16,1,6,768]{3,0,2,1:T(8,128)}, u32[]{:S(2)}, u32[]{:S(2)}) collective-permute-start(f32[16,1,6,768]{3,0,2,1:T(8,128)} %get-tuple-element.5), channel_id=1, source_target_pairs={{0,1},{1,2},{2,3},{3,4},{4,5},{5,6},{6,7},{7,8},{8,9},{9,10},{10,1... | collective-permute-start | bytes 884744 | tf_op jit(solution)/shard_map/ppermute | solution.py:15
  930.4 409.9 %collective-permute-start.5 = (f32[16,1,6,768]{3,0,2,1:T(8,128)}, f32[16,1,6,768]{3,0,2,1:T(8,128)}, u32[]{:S(2)}, u32[]{:S(2)}) collective-permute-start(f32[16,1,6,768]{3,0,2,1:T(8,128)} %get-tuple-element.8), channel_id=1, source_target_pairs={{1,0},{2,1},{3,2},{4,3},{5,4},{6,5},{7,6},{8,7},{9,8},{10,9},{11,1... | collective-permute-start | bytes 884744 | tf_op jit(solution)/shard_map/ppermute | solution.py:17
  1331.7 9.9 copy-start.7
  1331.7 9.9 copy-start.8
  1333.7 1.0 copy-start.3
Sparse Core Ops, SparseCore 0:
  26.5 409.8 all-reduce.3
  479.8 392.7 all-reduce.5
  925.9 392.7 all-reduce.7
where the time goes:
time: 1360 us
  waiting for transfers between devices  1170 us (86%)
  local copies, waits for them, and re-layouts  103 us (8%)
  other arithmetic  45.1 us (3%)
  starting transfers between devices  17.8 us (1%)
    psum x3, waiting for transfers between devices, gather_edges(): edge_set = lax.psum(rim_cells, 'ty')  1170 us
  transfers between devices with their start and end apart: 9, of which 3 were waited for; matrix products, arithmetic and copies ran while one was open for 5% of the time, Pallas kernels for 0%

commit v1 on v0

v1 whole, which is shorter than its diff:
```python
import functools

import jax
import jax.numpy as jnp
from jax import lax
from jax.experimental import pallas as pl
from jax.experimental.pallas import tpu as pltpu
from jax.sharding import PartitionSpec as P

MESH = pl.DeviceIdType.MESH
LANES = 128
PAD = 8
SOUTH, EAST, NORTH, WEST = 0, 1, 2, 3


def exact_dot(values, onehot):
    high = values.astype(jnp.bfloat16)
    rest = values - high.astype(jnp.float32)
    middle = rest.astype(jnp.bfloat16)
    low = (rest - middle.astype(jnp.float32)).astype(jnp.bfloat16)
    total = jnp.dot(low, onehot, preferred_element_type=jnp.float32)
    total = total + jnp.dot(middle, onehot, preferred_element_type=jnp.float32)
    return total + jnp.dot(high, onehot, preferred_element_type=jnp.float32)


def exact_left_dot(onehot, values):
    high = values.astype(jnp.bfloat16)
    rest = values - high.astype(jnp.float32)
    middle = rest.astype(jnp.bfloat16)
    low = (rest - middle.astype(jnp.float32)).astype(jnp.bfloat16)
    total = jnp.dot(onehot, low, preferred_element_type=jnp.float32)
    total = total + jnp.dot(onehot, middle, preferred_element_type=jnp.float32)
    return total + jnp.dot(onehot, high, preferred_element_type=jnp.float32)


def rows_reversed(block):
    count = block.shape[0]
    return jnp.concatenate([block[count - 1 - j : count - j] for j in range(count)], axis=0)


def level_eye(shape, code_row, source_code):
    row_lane = lax.broadcasted_iota(jnp.int32, shape, 0)
    column = lax.broadcasted_iota(jnp.int32, shape, 1)
    hit = (lax.shift_right_logical(row_lane, 3) == lax.shift_right_logical(column, 3)) & (
        code_row == jnp.bitwise_and(row_lane, 7) * 4 + source_code
    )
    return jnp.where(hit, 1.0, 0.0).astype(jnp.bfloat16)


def kernel(
    n, fields_hbm, metric_hbm, codes, damp_four, damp_six, out,
    f0, f1, f2, met, row_halo, own, mirror, piece_send, piece_all, piece_out, piece_in,
    stack, turned, rest_turned, extract, part, cell_metric, fix, fix_turned, k_halo, k_far,
    load_sem, row_send, row_recv, mir_send, mir_recv, far_send, far_recv, fan_send, fan_recv,
):
    levels, rows, faces, width = f0.shape
    blocks = width // LANES
    me = lax.axis_index("ty")
    last = n - 1
    at_first, at_last = me == 0, me == last
    special = jnp.logical_or(at_first, at_last)
    side = jnp.where(at_last, 1, 0)
    rim_row = side * (rows - 1)
    above, below = lax.rem(me + 1, n), lax.rem(me + last, n)
    opposite = last - me

    load_fields = pltpu.make_async_copy(fields_hbm, f0, load_sem.at[0])
    load_metric = pltpu.make_async_copy(metric_hbm, met, load_sem.at[1])
    load_fields.start()
    load_metric.start()

    barrier = pltpu.get_barrier_semaphore()

    def greet(device):
        pl.semaphore_signal(barrier, inc=1, device_id={"ty": device}, device_id_type=MESH)

    def spread(i):
        step = (i + 1) // 2
        return lax.rem(me + n // 2 + step * (1 - 2 * lax.rem(i, 2)) + n, n)

    @pl.when(special)
    def _():
        def one(i, _):
            greet(spread(i))
            return 0

        lax.fori_loop(0, last, one, 0)

    @pl.when(jnp.logical_not(at_first))
    def _():
        greet(0)

    @pl.when(jnp.logical_not(at_last))
    def _():
        greet(last)

    greet(above)
    greet(below)
    greet(opposite)

    stack[...] = jnp.zeros_like(stack)
    extract[...] = jnp.zeros_like(extract)
    fix[...] = jnp.zeros_like(fix)
    code_of = [codes[e : e + 1, :] for e in range(4)]
    reversed_south = codes[4:5, :] == 1
    reversed_north = codes[5:6, :] == 1
    square = (LANES, LANES)
    none = jnp.zeros(square, jnp.bfloat16)
    for index, (edge, to_west, to_east) in enumerate(
        ((WEST, 0, 1), (EAST, 1, 0), (WEST, 1, 0), (EAST, 0, 1), (SOUTH, 1, 1), (NORTH, 1, 1))
    ):
        span = slice(index * LANES, (index + 1) * LANES)
        k_halo[span, :LANES] = level_eye(square, code_of[WEST], edge) if to_west else none
        k_halo[span, LANES:] = level_eye(square, code_of[EAST], edge) if to_east else none
    for index, edge in enumerate((WEST, EAST)):
        span = slice(index * LANES, (index + 1) * LANES)
        k_far[span, :LANES] = level_eye(square, code_of[SOUTH], edge)
        k_far[span, LANES:] = level_eye(square, code_of[NORTH], edge)

    lane = lax.broadcasted_iota(jnp.int32, (faces, LANES), 1)
    wide_lane = lax.broadcasted_iota(jnp.int32, (faces, width), 1)

    def columns_of(west_tile, east_tile):
        total = jnp.zeros((faces, LANES), jnp.float32)
        for y in range(rows):
            total = jnp.where(lane == y, west_tile(y)[:, 0:1], total)
            total = jnp.where(lane == 16 + y, east_tile(y)[:, LANES - 1 : LANES], total)
        return total

    def turned_columns():
        table = extract[...].reshape(levels * PAD, LANES).T
        return table[0:rows], table[16 : 16 + rows]

    def take_columns(source):
        def one(level, _):
            extract[level, 0:faces, :] = columns_of(
                lambda y: source[level, y, :, 0:LANES],
                lambda y: source[level, y, :, width - LANES : width],
            )
            return 0

        lax.fori_loop(0, levels, one, 0)
        return turned_columns()

    def row_copy(round_, way):
        return pltpu.make_async_remote_copy(
            src_ref=(f0, f1, f2)[round_].at[:, 0 if way else rows - 1],
            dst_ref=row_halo.at[round_, way],
            send_sem=row_send.at[round_, way],
            recv_sem=row_recv.at[round_, way],
            device_id={"ty": below if way else above},
            device_id_type=MESH,
        )

    def mirror_copy(round_):
        return pltpu.make_async_remote_copy(
            src_ref=own.at[round_],
            dst_ref=mirror.at[round_],
            send_sem=mir_send.at[round_],
            recv_sem=mir_recv.at[round_],
            device_id={"ty": opposite},
            device_id_type=MESH,
        )

    def far_copy(round_, end):
        return pltpu.make_async_remote_copy(
            src_ref=piece_send.at[round_, end],
            dst_ref=piece_all.at[round_, me],
            send_sem=far_send.at[round_, end],
            recv_sem=far_recv.at[round_],
            device_id={"ty": last if end else 0},
            device_id_type=MESH,
        )

    def fan_copy(round_, device):
        return pltpu.make_async_remote_copy(
            src_ref=piece_out.at[round_, device],
            dst_ref=piece_in.at[round_, side],
            send_sem=fan_send.at[round_],
            recv_sem=fan_recv.at[round_, side],
            device_id={"ty": device},
            device_id_type=MESH,
        )

    def all_but_one(buffer, sem):
        return pltpu.make_async_copy(buffer.at[pl.ds(0, last)], buffer.at[pl.ds(0, last)], sem)

    def make_far_pieces(round_):
        west, east = own[round_, 0], own[round_, 1]
        straight = jnp.concatenate([west, east], axis=1)
        both = jnp.concatenate([straight, rows_reversed(straight)], axis=0)
        chosen = exact_dot(both, k_far[...])
        for end, flag in ((0, reversed_south), (1, reversed_north)):
            span = slice(end * LANES, (end + 1) * LANES)
            piece_send[round_, end] = jnp.where(flag, chosen[rows:, span], chosen[:rows, span])

    def send_columns(round_):
        mirror_copy(round_).start()
        make_far_pieces(round_)

        @pl.when(jnp.logical_not(at_first))
        def _():
            far_copy(round_, 0).start()

        @pl.when(jnp.logical_not(at_last))
        def _():
            far_copy(round_, 1).start()

        @pl.when(special)
        def _():
            piece_all[round_, me] = jnp.where(at_last, piece_send[round_, 1], piece_send[round_, 0])

    def send_rows(round_):
        row_copy(round_, 0).start()
        row_copy(round_, 1).start()

    def turn_stack(target):
        for b in range(blocks):
            span = slice(b * LANES, (b + 1) * LANES)
            target[span, :] = stack[:, :, span].reshape(levels * PAD, LANES).T

    def pack_fan(round_, source):
        stack[:, 0:faces, :] = source[:, rim_row]
        turn_stack(turned)
        flag = codes[pl.ds(4 + side, 1), :] == 1
        for j in range(n):
            here = turned[rows * j : rows * (j + 1), :]
            there = turned[rows * (last - j) : rows * (n - j), :]
            piece_out[round_, j] = jnp.where(flag, there, here)

        def one(i, _):
            fan_copy(round_, spread(i)).start()
            return 0

        lax.fori_loop(0, last, one, 0)
        piece_in[round_, side] = piece_out[round_, me]

    def local_seams(round_):
        code = codes[pl.ds(2 * side, 1), :]
        same = level_eye(square, code, 2 * side)
        other = level_eye(square, code, 2 - 2 * side)
        up = lax.broadcasted_iota(jnp.int32, square, 0)
        across = lax.broadcasted_iota(jnp.int32, square, 1)
        flip = jnp.where(up + across == LANES - 1, 1.0, 0.0).astype(jnp.bfloat16)
        stack[:, 0:faces, :] = row_halo[round_, side]
        turn_stack(rest_turned)
        for b in range(blocks):
            span = slice(b * LANES, (b + 1) * LANES)
            back = slice((blocks - 1 - b) * LANES, (blocks - b) * LANES)
            flipped = exact_left_dot(flip, turned[back, :])
            rest_turned[span, :] = exact_dot(flipped, same) + exact_dot(rest_turned[span, :], other)

    def join_far(round_):
        flag = codes[pl.ds(4 + side, 1), :] == 1
        for j in range(n):
            span = slice(rows * j, rows * (j + 1))
            rest_turned[span, :] += jnp.where(flag, piece_all[round_, last - j], piece_all[round_, j])
        for b in range(blocks):
            span = slice(b * LANES, (b + 1) * LANES)
            stack[:, :, span] = rest_turned[span, :].T.reshape(levels, PAD, LANES)

    def apply_interior(source, target, final):
        def one(level, _):
            cells = [source[level, y] for y in range(rows)]
            for y in range(rows):
                here = cells[y]
                west = jnp.where(wide_lane == 0, 0.0, pltpu.roll(here, 1, 1))
                east = jnp.where(wide_lane == width - 1, 0.0, pltpu.roll(here, width - 1, 1))
                south = cells[y - 1] if y > 0 else jnp.zeros_like(here)
                north = cells[y + 1] if y < rows - 1 else jnp.zeros_like(here)
                value = (
                    met[0, y] * (west - here)
                    + met[1, y] * (east - here)
                    + met[2, y] * (south - here)
                    + met[3, y] * (north - here)
                )
                if final:
                    value = f0[level, y] - damp_four[level] * here + damp_six[level] * value
                target[level, y] = value
            return 0

        lax.fori_loop(0, levels, one, 0)

    def add_row(target, y, weight, halo, final):
        def one(level, _):
            value = met[weight, y] * halo(level)
            if final:
                value = damp_six[level] * value
            target[level, y] += value
            return 0

        lax.fori_loop(0, levels, one, 0)

    def add_columns(target, which, final):
        def one(level, _):
            table = fix_turned[level, 0:faces, :]
            if final:
                table = table * damp_six[level]
            for y in which:
                target[level, y, :, 0:LANES] += jnp.where(lane == 0, table[:, y : y + 1], 0.0)
                target[level, y, :, width - LANES : width] += jnp.where(
                    lane == LANES - 1, table[:, 16 + y : 17 + y], 0.0
                )
            return 0

        lax.fori_loop(0, levels, one, 0)

    load_fields.wait()
    west, east = take_columns(f0)
    own[0, 0] = west
    own[0, 1] = east
    load_metric.wait()
    weights = columns_of(
        lambda y: met[0, y, :, 0:LANES], lambda y: met[1, y, :, width - LANES : width]
    )
    for level in range(levels):
        extract[level, 0:faces, :] = weights
    west, east = turned_columns()
    cell_metric[0] = west
    cell_metric[1] = east

    pl.semaphore_wait(
        barrier,
        3 + jnp.where(at_first, last, 1) + jnp.where(at_last, last, 1),
    )

    send_columns(0)
    send_rows(0)

    @pl.when(special)
    def _():
        pack_fan(0, f0)

    for round_ in range(3):
        source = (f0, f1, f2)[round_]
        target = (f1, f2, out)[round_]
        final = round_ == 2
        apply_interior(source, target, final)

        row_copy(round_, 0).wait_recv()
        row_copy(round_, 1).wait_recv()

        @pl.when(jnp.logical_not(at_first))
        def _():
            add_row(target, 0, 2, lambda level: row_halo[round_, 0, level], final)

        @pl.when(jnp.logical_not(at_last))
        def _():
            add_row(target, rows - 1, 3, lambda level: row_halo[round_, 1, level], final)

        @pl.when(special)
        def _():
            local_seams(round_)
            all_but_one(piece_all.at[round_], far_recv.at[round_]).wait()
            join_far(round_)
            add_row(target, rim_row, 2 + side, lambda level: stack[level, 0:faces, :], final)

        if not final:
            west, east = take_columns(target)
            part[0] = west
            part[1] = east

        mirror_copy(round_).wait_recv()

        @pl.when(jnp.logical_not(at_first))
        def _():
            pltpu.make_async_copy(piece_in.at[round_, 0], piece_in.at[round_, 0], fan_recv.at[round_, 0]).wait()

        @pl.when(jnp.logical_not(at_last))
        def _():
            pltpu.make_async_copy(piece_in.at[round_, 1], piece_in.at[round_, 1], fan_recv.at[round_, 1]).wait()

        from_south, from_north = piece_in[round_, 0], piece_in[round_, 1]
        candidates = jnp.concatenate(
            [
                own[round_, 0],
                own[round_, 1],
                rows_reversed(mirror[round_, 0]),
                rows_reversed(mirror[round_, 1]),
                jnp.where(reversed_south, rows_reversed(from_south), from_south),
                jnp.where(reversed_north, rows_reversed(from_north), from_north),
            ],
            axis=1,
        )
        halo = exact_dot(candidates, k_halo[...])
        west = cell_metric[0] * halo[:, :LANES]
        east = cell_metric[1] * halo[:, LANES:]
        if not final:
            own[round_ + 1, 0] = part[0] + west
            own[round_ + 1, 1] = part[1] + east
            send_columns(round_ + 1)
        fix[0:rows, :] = west
        fix[16 : 16 + rows, :] = east
        fix_turned[...] = fix[...].T.reshape(levels, PAD, LANES)
        if final:
            add_columns(target, range(rows), True)
        else:
            add_columns(target, (0, rows - 1), False)
            send_rows(round_ + 1)

            @pl.when(special)
            def _():
                pack_fan(round_ + 1, target)

            add_columns(target, range(1, rows - 1), False)

    for round_ in range(3):
        row_copy(round_, 0).wait_send()
        row_copy(round_, 1).wait_send()
        mirror_copy(round_).wait_send()

        @pl.when(jnp.logical_not(at_first))
        def _():
            far_copy(round_, 0).wait_send()

        @pl.when(jnp.logical_not(at_last))
        def _():
            far_copy(round_, 1).wait_send()

        @pl.when(special)
        def _():
            all_but_one(piece_out.at[round_], fan_send.at[round_]).wait()


def code_rows(seam_table, levels):
    joined = seam_table[:, :, 0] * 4 + seam_table[:, :, 1]
    table = jnp.concatenate([joined.T, seam_table[:, 0:3:2, 2].T], axis=0)
    table = jnp.pad(table, ((0, 2), (0, PAD - table.shape[1])), constant_values=-1)
    return jnp.tile(table, (1, levels))


def solution(mesh):
    n = mesh.shape["ty"]

    def per_device(fields, damp_four, damp_six, metric, seam_table):
        levels, rows, faces, width = fields.shape
        f32, bf16 = jnp.float32, jnp.bfloat16
        vmem, dma = pltpu.VMEM, pltpu.SemaphoreType.DMA
        any_space = pl.BlockSpec(memory_space=pl.ANY)
        in_smem = pl.BlockSpec(memory_space=pltpu.SMEM)
        in_vmem = pl.BlockSpec(memory_space=pltpu.VMEM)
        return pl.pallas_call(
            functools.partial(kernel, n),
            out_shape=jax.ShapeDtypeStruct(fields.shape, f32),
            in_specs=[any_space, any_space, in_vmem, in_smem, in_smem],
            out_specs=in_vmem,
            scratch_shapes=[
                vmem(fields.shape, f32),
                vmem(fields.shape, f32),
                vmem(fields.shape, f32),
                vmem(metric.shape, f32),
                vmem((3, 2, levels, faces, width), f32),
                vmem((3, 2, rows, LANES), f32),
                vmem((3, 2, rows, LANES), f32),
                vmem((3, 2, rows, LANES), f32),
                vmem((3, n, rows, LANES), f32),
                vmem((3, n, rows, LANES), f32),
                vmem((3, 2, rows, LANES), f32),
                vmem((levels, PAD, width), f32),
                vmem((width, LANES), f32),
                vmem((width, LANES), f32),
                vmem((levels, PAD, LANES), f32),
                vmem((2, rows, LANES), f32),
                vmem((2, rows, LANES), f32),
                vmem((LANES, LANES), f32),
                vmem((levels, PAD, LANES), f32),
                vmem((6 * LANES, 2 * LANES), bf16),
                vmem((2 * LANES, 2 * LANES), bf16),
                dma((2,)),
                dma((3, 2)),
                dma((3, 2)),
                dma((3,)),
                dma((3,)),
                dma((3, 2)),
                dma((3,)),
                dma((3,)),
                dma((3, 2)),
            ],
            compiler_params=pltpu.CompilerParams(
                collective_id=0, has_side_effects=True, vmem_limit_bytes=60 * 1024 * 1024
            ),
        )(fields, metric, code_rows(seam_table, levels), damp_four, damp_six)

    placed = (
        P("member", "ty", None, None),
        P("member"),
        P("member"),
        P(None, "ty", None, None),
        P(),
    )
    return jax.shard_map(
        per_device,
        mesh=mesh,
        in_specs=placed,
        out_specs=P("member", "ty", None, None),
        check_vma=False,
    )
```

time: 1360 us -> 99.4 us (0.07)
  waiting for transfers between devices: 1170 us -> 0 us
  local copies, waits for them, and re-layouts: 103 us -> 16.2 us
  Pallas kernels: 0 us -> 82.1 us
  other arithmetic: 45.1 us -> 0.71 us
  starting transfers between devices: 17.8 us -> 0 us
    psum x3 -> x0, waiting for transfers between devices: 1170 us -> none  [gather_edges(): edge_set = lax.psum(rim_cells, 'ty')]
    pallas_call x0 -> x1, Pallas kernels: none -> 82.1 us  [per_device(): pl.pallas_call(functools.partial(kernel, n), out_shape=jax.ShapeDtypeStru...]
    add x4 -> x0, other arithmetic: 24.7 us -> none  [the longest x2 14.1 us: laplace(): metric[0] * (padded_x[..., :-2] - source)]
    slice x13 -> x1, local copies, waits for them, and re-layouts: 21.4 us -> 0.7 us  [code_rows(): table = jnp.concatenate([joined.T, seam_table[:, 0:3:2, 2].T], axis=0)]
    reshape x8 -> x0, local copies, waits for them, and re-layouts: 19.8 us -> none  [the longest x5 11.9 us: seam_halo(): neighbor = neighbor.reshape(levels, 6, 4, row_width)]
    broadcast_in_dim x11 -> x0, local copies, waits for them, and re-layouts: 19.7 us -> none  [the longest x6 11.2 us: laplace(): jnp.transpose(lax.dynamic_slice_in_dim(halo_cells[:, :, 1], row_start, st...]
    ppermute x6 -> x0, starting transfers between devices: 17.6 us -> none  [the longest x3 13.3 us: with_halo(): lax.ppermute(tail, axis, [(i, (i + 1) % count) for i in range(ends)])]
    rev x3 -> x0, local copies, waits for them, and re-layouts: 14.1 us -> none  [seam_halo(): return jnp.where(flipped, neighbor[..., ::-1], neighbor)]
  transfers between devices with their start and end apart: 9 -> 0, of which waited for: 3 -> 0; matrix products, arithmetic and copies ran while one was open for 5% -> 0% of each run, Pallas kernels for 0% -> 0%
where the time goes in v1:
time: 99.4 us; the launch traced here: 99.1 us
  Pallas kernels  82.1 us (83%)
  local copies, waits for them, and re-layouts  16.2 us (16%)
    pallas_call x1, Pallas kernels, per_device(): pl.pallas_call(functools.partial(kernel, n), out_shape=jax.ShapeDtypeStru...  82.1 us
    unnamed x2, local copies, waits for them, and re-layouts  8.66 us
    pallas_call x1, local copies, waits for them, and re-layouts, per_device(): pl.pallas_call(functools.partial(kernel, n), out_shape=jax.ShapeDtypeStru...  6.18 us

profile of v1, /device:TPU:38, one launch (start us, length us, event | category | flops | bytes accessed | tf_op | source)
XLA Modules:
  0.0 99.1 jit_solution(1180392966008666873)
XLA Ops:
  0.0 0.7 slice.11
  0.7 0.7 add_bitcast_fusion
  1.4 0.7 tile.10.codes
  2.1 2.4 %copy.10.metric_hbm = f32[4,12,6,768]{3,2,1,0:T(8,128)} copy(f32[4,12,6,768]{3,0,2,1:T(4,128)} %param.8) | data formatting | bytes 1769472 | tf_op args[3]
  4.5 6.2 %copy.9.fields_hbm = f32[16,12,6,768]{3,2,1,0:T(8,128)} copy(f32[16,12,6,768]{3,0,2,1:T(8,128)} %param.5) | data formatting | bytes 7077888 | tf_op args[0]
  10.8 82.1 %shard_map.55 = f32[16,12,6,768]{3,2,1,0:T(8,128)} custom-call(f32[16,12,6,768]{3,2,1,0:T(8,128)} %copy.9.fields_hbm, f32[4,12,6,768]{3,2,1,0:T(8,128)} %copy.10.metric_hbm, s32[8,128]{1,0:T(8,128)} %tile.10.codes, f32[16]{0:T(128)} %damp_four.1, f32[16]{0:T(128)} %damp_six.1), custom_call_target="tpu_custom_call" | custom-call | tf_op jit(solution)/shard_map/pallas_call | solution.py:442
  92.9 6.2 %copy.11 = f32[16,12,6,768]{3,0,2,1:T(8,128)} copy(f32[16,12,6,768]{3,2,1,0:T(8,128)} %shard_map.55) | data formatting | bytes 7077888 | tf_op jit(solution)/shard_map/pallas_call | solution.py:442
  (3 shorter events, 0.0 us)

commit v2 on v1

v2 whole, which is shorter than its diff:
```python
import functools

import jax
import jax.numpy as jnp
from jax import lax
from jax.experimental import pallas as pl
from jax.experimental.pallas import tpu as pltpu
from jax.sharding import PartitionSpec as P

MESH = pl.DeviceIdType.MESH
LANES = 128
PAD = 8
SOUTH, EAST, NORTH, WEST = 0, 1, 2, 3


def three_parts(values):
    high = values.astype(jnp.bfloat16).astype(jnp.float32)
    rest = values - high
    middle = rest.astype(jnp.bfloat16).astype(jnp.float32)
    return high, middle, rest - middle


def exact_dot(values, onehot):
    count = values.shape[0]
    short = -count % 8
    if short:
        values = jnp.concatenate([values, jnp.zeros((short, values.shape[1]), jnp.float32)], axis=0)
    whole = count + short
    stacked = jnp.concatenate(three_parts(values), axis=0).astype(jnp.bfloat16)
    product = jnp.dot(stacked, onehot, preferred_element_type=jnp.float32)
    total = product[2 * whole :] + product[whole : 2 * whole] + product[:whole]
    return total[:count]


def exact_left_dot(onehot, values):
    wide = values.shape[1]
    stacked = jnp.concatenate(three_parts(values), axis=1).astype(jnp.bfloat16)
    product = jnp.dot(onehot, stacked, preferred_element_type=jnp.float32)
    return product[:, 2 * wide :] + product[:, wide : 2 * wide] + product[:, :wide]


def rows_reversed(block):
    count = block.shape[0]
    return jnp.concatenate([block[count - 1 - j : count - j] for j in range(count)], axis=0)


def level_eye(shape, code_row, source_code, shift):
    row_lane = lax.broadcasted_iota(jnp.int32, shape, 0)
    column = lax.broadcasted_iota(jnp.int32, shape, 1)
    level = (1 << shift) - 1
    hit = (jnp.bitwise_and(row_lane, level) == jnp.bitwise_and(column, level)) & (
        code_row == lax.shift_right_logical(row_lane, shift) * 4 + source_code
    )
    return jnp.where(hit, 1.0, 0.0).astype(jnp.bfloat16)


def kernel(
    n, fields_hbm, metric_hbm, seam, damp_four, damp_six, out_hbm,
    f0, f1, f2, out, met, row_halo, own, mirror, piece_send, piece_all, piece_out, piece_in,
    stack, turned, turned_part, rim_weight, rest, extract, part, cell_metric, corner_metric,
    fix, fix_turned, k_halo, k_far, codes, damp,
    load_sem, store_sem, row_send, row_recv, mir_send, mir_recv, far_send, far_recv, fan_send, fan_recv,
):
    rows, faces, levels, width = f0.shape
    shift = levels.bit_length() - 1
    blocks = width // LANES
    me = lax.axis_index("ty")
    last = n - 1
    at_first, at_last = me == 0, me == last
    special = jnp.logical_or(at_first, at_last)
    side = jnp.where(at_last, 1, 0)
    rim_row = side * (rows - 1)
    above, below = lax.rem(me + 1, n), lax.rem(me + last, n)
    opposite = last - me

    load_fields = pltpu.make_async_copy(fields_hbm, f0, load_sem.at[0])
    load_metric = pltpu.make_async_copy(metric_hbm, met, load_sem.at[1])
    load_fields.start()
    load_metric.start()

    barrier = pltpu.get_barrier_semaphore()

    def greet(device):
        pl.semaphore_signal(barrier, inc=1, device_id={"ty": device}, device_id_type=MESH)

    def spread(i):
        step = (i + 1) // 2
        return lax.rem(me + n // 2 + step * (1 - 2 * lax.rem(i, 2)) + n, n)

    @pl.when(special)
    def _():
        def one(i, _):
            greet(spread(i))
            return 0

        lax.fori_loop(0, last, one, 0)

    @pl.when(jnp.logical_not(at_first))
    def _():
        greet(0)

    @pl.when(jnp.logical_not(at_last))
    def _():
        greet(last)

    greet(above)
    greet(below)
    greet(opposite)

    stack[...] = jnp.zeros_like(stack)
    extract[...] = jnp.zeros_like(extract)
    fix[...] = jnp.zeros_like(fix)
    face_of_lane = lax.shift_right_logical(lax.broadcasted_iota(jnp.int32, (1, LANES), 1), shift)

    def lane_row(entry):
        total = jnp.full((1, LANES), -1, jnp.int32)
        for face in range(faces):
            total = jnp.where(face_of_lane == face, entry(face), total)
        return total

    code_of = [lane_row(lambda f, e=e: seam[0, e, f] * 4 + seam[1, e, f]) for e in range(4)]
    flags = [lane_row(lambda f, e=e: seam[2, e, f]) for e in (SOUTH, NORTH)]
    for index, row in enumerate((code_of[SOUTH], code_of[NORTH], flags[0], flags[1])):
        codes[index : index + 1, :] = row
    reversed_south, reversed_north = flags[0] == 1, flags[1] == 1
    square = (LANES, LANES)
    none = jnp.zeros(square, jnp.bfloat16)
    for index, (edge, to_west, to_east) in enumerate(
        ((WEST, 0, 1), (EAST, 1, 0), (WEST, 1, 0), (EAST, 0, 1), (SOUTH, 1, 1), (NORTH, 1, 1))
    ):
        span = slice(index * LANES, (index + 1) * LANES)
        k_halo[span, :LANES] = level_eye(square, code_of[WEST], edge, shift) if to_west else none
        k_halo[span, LANES:] = level_eye(square, code_of[EAST], edge, shift) if to_east else none
    for index, edge in enumerate((WEST, EAST)):
        span = slice(index * LANES, (index + 1) * LANES)
        k_far[span, :LANES] = level_eye(square, code_of[SOUTH], edge, shift)
        k_far[span, LANES:] = level_eye(square, code_of[NORTH], edge, shift)
    level_row = lax.broadcasted_iota(jnp.int32, (levels, LANES), 0)
    for index, source in enumerate((damp_four, damp_six)):
        total = jnp.zeros((levels, LANES), jnp.float32)
        for level in range(levels):
            total = jnp.where(level_row == level, source[level], total)
        damp[index] = total

    lane = lax.broadcasted_iota(jnp.int32, (levels, LANES), 1)
    wide_lane = lax.broadcasted_iota(jnp.int32, (8, width), 1)

    def columns_of(west_tile, east_tile):
        total = jnp.zeros((levels, LANES), jnp.float32)
        for y in range(rows):
            total = jnp.where(lane == y, west_tile(y), total)
            total = jnp.where(lane == 16 + y, east_tile(y), total)
        return total

    def turned_columns():
        return extract[...].reshape(LANES, LANES).T

    def take_columns(source):
        def one(face, _):
            extract[face] = columns_of(
                lambda y: source[y, face, :, 0:LANES][:, 0:1],
                lambda y: source[y, face, :, width - LANES : width][:, LANES - 1 : LANES],
            )
            return 0

        lax.fori_loop(0, faces, one, 0)
        table = turned_columns()
        return table[0:rows], table[16 : 16 + rows]

    def row_copy(round_, way):
        return pltpu.make_async_remote_copy(
            src_ref=(f0, f1, f2)[round_].at[0 if way else rows - 1],
            dst_ref=row_halo.at[round_, way],
            send_sem=row_send.at[round_, way],
            recv_sem=row_recv.at[round_, way],
            device_id={"ty": below if way else above},
            device_id_type=MESH,
        )

    def mirror_copy(round_):
        return pltpu.make_async_remote_copy(
            src_ref=own.at[round_],
            dst_ref=mirror.at[round_],
            send_sem=mir_send.at[round_],
            recv_sem=mir_recv.at[round_],
            device_id={"ty": opposite},
            device_id_type=MESH,
        )

    def far_copy(round_, end):
        return pltpu.make_async_remote_copy(
            src_ref=piece_send.at[round_, end],
            dst_ref=piece_all.at[round_, me],
            send_sem=far_send.at[round_, end],
            recv_sem=far_recv.at[round_],
            device_id={"ty": last if end else 0},
            device_id_type=MESH,
        )

    def fan_copy(round_, device):
        return pltpu.make_async_remote_copy(
            src_ref=piece_out.at[round_, device],
            dst_ref=piece_in.at[round_, side],
            send_sem=fan_send.at[round_],
            recv_sem=fan_recv.at[round_, side],
            device_id={"ty": device},
            device_id_type=MESH,
        )

    def all_but_one(buffer, sem):
        return pltpu.make_async_copy(buffer.at[pl.ds(0, last)], buffer.at[pl.ds(0, last)], sem)

    def make_far_pieces(round_):
        straight = jnp.concatenate([own[round_, 0], own[round_, 1]], axis=1)
        both = jnp.concatenate([straight, rows_reversed(straight)], axis=0)
        chosen = exact_dot(both, k_far[...])
        for end, flag in ((0, reversed_south), (1, reversed_north)):
            span = slice(end * LANES, (end + 1) * LANES)
            piece_send[round_, end] = jnp.where(flag, chosen[rows:, span], chosen[:rows, span])

    def send_columns(round_):
        @pl.when(jnp.logical_not(at_first))
        def _():
            far_copy(round_, 0).start()

        @pl.when(jnp.logical_not(at_last))
        def _():
            far_copy(round_, 1).start()

        mirror_copy(round_).start()

        @pl.when(special)
        def _():
            piece_all[round_, me] = jnp.where(at_last, piece_send[round_, 1], piece_send[round_, 0])

    def send_rows(round_):
        row_copy(round_, 0).start()
        row_copy(round_, 1).start()

    def turn_into(target, planes):
        stack[0:faces] = planes
        for b in range(blocks):
            span = slice(b * LANES, (b + 1) * LANES)
            target[span, :] = stack[:, :, span].reshape(LANES, LANES).T

    def pack_fan(round_):
        flag = codes[pl.ds(2 + side, 1), :] == 1
        for j in range(n):
            here = turned[rows * j : rows * (j + 1), :]
            there = turned[rows * (last - j) : rows * (n - j), :]
            piece_out[round_, j] = jnp.where(flag, there, here)

    def send_fan(round_):
        def one(i, _):
            fan_copy(round_, spread(i)).start()
            return 0

        lax.fori_loop(0, last, one, 0)
        piece_in[round_, side] = piece_out[round_, me]

    def local_seams(round_):
        code = codes[pl.ds(side, 1), :]
        same = level_eye(square, code, 2 * side, shift)
        other = level_eye(square, code, 2 - 2 * side, shift)
        up = lax.broadcasted_iota(jnp.int32, square, 0)
        across = lax.broadcasted_iota(jnp.int32, square, 1)
        flip = jnp.where(up + across == LANES - 1, 1.0, 0.0).astype(jnp.bfloat16)
        turn_into(rest, row_halo[round_, side])
        for b in range(blocks):
            span = slice(b * LANES, (b + 1) * LANES)
            back = slice((blocks - 1 - b) * LANES, (blocks - b) * LANES)
            flipped = exact_left_dot(flip, turned[back, :])
            rest[span, :] = exact_dot(flipped, same) + exact_dot(rest[span, :], other)

    def join_far(round_):
        flag = codes[pl.ds(2 + side, 1), :] == 1
        for j in range(n):
            span = slice(rows * j, rows * (j + 1))
            rest[span, :] += jnp.where(flag, piece_all[round_, last - j], piece_all[round_, j])

    def apply_interior(source, target, final):
        halves = levels // 8

        def one(step, _):
            face = step // halves
            some = pl.ds(pl.multiple_of(lax.rem(step, halves) * 8, 8), 8)
            cells = [source[y, face, some, :] for y in range(rows)]
            if final:
                four = jnp.concatenate([damp[0, some, :]] * blocks, axis=1)
                six = jnp.concatenate([damp[1, some, :]] * blocks, axis=1)
            for y in range(rows):
                here = cells[y]
                west = jnp.where(wide_lane == 0, 0.0, pltpu.roll(here, 1, 1))
                east = jnp.where(wide_lane == width - 1, 0.0, pltpu.roll(here, width - 1, 1))
                south = cells[y - 1] if y > 0 else jnp.zeros_like(here)
                north = cells[y + 1] if y < rows - 1 else jnp.zeros_like(here)
                value = (
                    met[y, face, 0:1, :] * (west - here)
                    + met[y, face, 1:2, :] * (east - here)
                    + met[y, face, 2:3, :] * (south - here)
                    + met[y, face, 3:4, :] * (north - here)
                )
                if final:
                    value = f0[y, face, some, :] - four * here + six * value
                target[y, face, some, :] = value
            return 0

        lax.fori_loop(0, faces * halves, one, 0)

    def add_row(target, y, weight, halo, final):
        def one(face, _):
            value = met[y, face, pl.ds(weight, 1), :] * halo(face)
            if final:
                value = jnp.concatenate([damp[1]] * blocks, axis=1) * value
            target[y, face] += value
            return 0

        lax.fori_loop(0, faces, one, 0)

    def add_columns(target, which, final):
        def one(face, _):
            table = fix_turned[face]
            if final:
                table = table * damp[1]
            for y in which:
                target[y, face, :, 0:LANES] += jnp.where(lane == 0, table[:, y : y + 1], 0.0)
                target[y, face, :, width - LANES : width] += jnp.where(
                    lane == LANES - 1, table[:, 16 + y : 17 + y], 0.0
                )
            return 0

        lax.fori_loop(0, faces, one, 0)

    middle = pl.ds(LANES, width - 2 * LANES)

    def store_copy(index):
        if index == 0:
            span = (pl.ds(1, rows - 2), slice(None), slice(None), middle)
        elif index < 3:
            span = ((0, rows - 1)[index - 1], slice(None), slice(None), middle)
        else:
            span = (slice(None), slice(None), slice(None), pl.ds((0, width - LANES)[index - 3], LANES))
        return pltpu.make_async_copy(out.at[span], out_hbm.at[span], store_sem.at[index])

    load_fields.wait()
    west, east = take_columns(f0)
    own[0, 0] = west
    own[0, 1] = east
    make_far_pieces(0)
    load_metric.wait()
    for face in range(faces):
        weights = columns_of(
            lambda y: met[y, face, 0:1, 0:LANES][:, 0:1],
            lambda y: met[y, face, 1:2, width - LANES : width][:, LANES - 1 : LANES],
        )
        rim = met[rim_row, face, pl.ds(2 + side, 1), :]
        weights = jnp.where(lane == 32, rim[:, 0:1], weights)
        extract[face] = jnp.where(lane == 33, rim[:, width - 1 : width], weights)
    table = turned_columns()
    cell_metric[0] = table[0:rows]
    cell_metric[1] = table[16 : 16 + rows]
    corner_metric[0] = table[32:33]
    corner_metric[1] = table[33:34]

    @pl.when(special)
    def _():
        for face in range(faces):
            stack[face] = jnp.broadcast_to(met[rim_row, face, pl.ds(2 + side, 1), :], (levels, width))
        for b in range(blocks):
            span = slice(b * LANES, (b + 1) * LANES)
            rim_weight[span, :] = stack[:, :, span].reshape(LANES, LANES).T
        turn_into(turned, f0[rim_row])
        pack_fan(0)

    pl.semaphore_wait(
        barrier,
        3 + jnp.where(at_first, last, 1) + jnp.where(at_last, last, 1),
    )

    send_columns(0)

    @pl.when(special)
    def _():
        send_fan(0)

    send_rows(0)

    for round_ in range(3):
        source = (f0, f1, f2)[round_]
        target = (f1, f2, out)[round_]
        final = round_ == 2
        apply_interior(source, target, final)
        if final:
            store_copy(0).start()

        row_copy(round_, 0).wait_recv()
        row_copy(round_, 1).wait_recv()

        @pl.when(jnp.logical_not(at_first))
        def _():
            add_row(target, 0, 2, lambda face: row_halo[round_, 0, face], final)

        @pl.when(jnp.logical_not(at_last))
        def _():
            add_row(target, rows - 1, 3, lambda face: row_halo[round_, 1, face], final)

        if not final:
            west, east = take_columns(target)
            part[0] = west
            part[1] = east

        @pl.when(special)
        def _():
            local_seams(round_)
            if not final:
                turn_into(turned_part, target[rim_row])
            all_but_one(piece_all.at[round_], far_recv.at[round_]).wait()
            join_far(round_)
            if not final:
                part[0, pl.ds(rim_row, 1), :] += corner_metric[0] * rest[0:1, :]
                part[1, pl.ds(rim_row, 1), :] += corner_metric[1] * rest[width - 1 : width, :]

        mirror_copy(round_).wait_recv()

        @pl.when(jnp.logical_not(at_first))
        def _():
            pltpu.make_async_copy(piece_in.at[round_, 0], piece_in.at[round_, 0], fan_recv.at[round_, 0]).wait()

        @pl.when(jnp.logical_not(at_last))
        def _():
            pltpu.make_async_copy(piece_in.at[round_, 1], piece_in.at[round_, 1], fan_recv.at[round_, 1]).wait()

        from_south, from_north = piece_in[round_, 0], piece_in[round_, 1]
        candidates = jnp.concatenate(
            [
                own[round_, 0],
                own[round_, 1],
                rows_reversed(mirror[round_, 0]),
                rows_reversed(mirror[round_, 1]),
                jnp.where(reversed_south, rows_reversed(from_south), from_south),
                jnp.where(reversed_north, rows_reversed(from_north), from_north),
            ],
            axis=1,
        )
        halo = exact_dot(candidates, k_halo[...])
        west = cell_metric[0] * halo[:, :LANES]
        east = cell_metric[1] * halo[:, LANES:]
        fix[0:rows, :] = west
        fix[16 : 16 + rows, :] = east
        if not final:
            own[round_ + 1, 0] = part[0] + west
            own[round_ + 1, 1] = part[1] + east
            make_far_pieces(round_ + 1)
            send_columns(round_ + 1)

            @pl.when(special)
            def _():
                turned[...] = turned_part[...] + rim_weight[...] * rest[...]
                turned[0:1, :] += fix[pl.ds(rim_row, 1), :]
                turned[width - 1 : width, :] += fix[pl.ds(16 + rim_row, 1), :]
                pack_fan(round_ + 1)
                send_fan(round_ + 1)

        @pl.when(special)
        def _():
            for b in range(blocks):
                span = slice(b * LANES, (b + 1) * LANES)
                stack[:, :, span] = rest[span, :].T.reshape(PAD, levels, LANES)
            add_row(target, rim_row, 2 + side, lambda face: stack[face], final)

        fix_turned[...] = fix[...].T.reshape(PAD, levels, LANES)
        if final:
            store_copy(1).start()
            store_copy(2).start()
            add_columns(target, range(rows), True)
            store_copy(3).start()
            store_copy(4).start()
        else:
            add_columns(target, (0, rows - 1), False)
            send_rows(round_ + 1)
            add_columns(target, range(1, rows - 1), False)

    for round_ in range(3):
        row_copy(round_, 0).wait_send()
        row_copy(round_, 1).wait_send()
        mirror_copy(round_).wait_send()

        @pl.when(jnp.logical_not(at_first))
        def _():
            far_copy(round_, 0).wait_send()

        @pl.when(jnp.logical_not(at_last))
        def _():
            far_copy(round_, 1).wait_send()

        @pl.when(special)
        def _():
            all_but_one(piece_out.at[round_], fan_send.at[round_]).wait()

    for index in range(5):
        store_copy(index).wait()


def solution(mesh):
    n = mesh.shape["ty"]

    def per_device(fields, damp_four, damp_six, metric, seam_table):
        fields = jnp.transpose(fields, (1, 2, 0, 3))
        metric = jnp.transpose(metric, (1, 2, 0, 3))
        rows, faces, levels, width = fields.shape
        f32, bf16 = jnp.float32, jnp.bfloat16
        vmem, dma = pltpu.VMEM, pltpu.SemaphoreType.DMA
        any_space = pl.BlockSpec(memory_space=pl.ANY)
        in_smem = pl.BlockSpec(memory_space=pltpu.SMEM)
        result = pl.pallas_call(
            functools.partial(kernel, n),
            out_shape=jax.ShapeDtypeStruct(fields.shape, f32),
            in_specs=[any_space, any_space, in_smem, in_smem, in_smem],
            out_specs=any_space,
            scratch_shapes=[
                vmem(fields.shape, f32),
                vmem(fields.shape, f32),
                vmem(fields.shape, f32),
                vmem(fields.shape, f32),
                vmem(metric.shape, f32),
                vmem((3, 2, faces, levels, width), f32),
                vmem((3, 2, rows, LANES), f32),
                vmem((3, 2, rows, LANES), f32),
                vmem((3, 2, rows, LANES), f32),
                vmem((3, n, rows, LANES), f32),
                vmem((3, n, rows, LANES), f32),
                vmem((3, 2, rows, LANES), f32),
                vmem((PAD, levels, width), f32),
                vmem((width, LANES), f32),
                vmem((width, LANES), f32),
                vmem((width, LANES), f32),
                vmem((width, LANES), f32),
                vmem((PAD, levels, LANES), f32),
                vmem((2, rows, LANES), f32),
                vmem((2, rows, LANES), f32),
                vmem((2, 1, LANES), f32),
                vmem((LANES, LANES), f32),
                vmem((PAD, levels, LANES), f32),
                vmem((6 * LANES, 2 * LANES), bf16),
                vmem((2 * LANES, 2 * LANES), bf16),
                vmem((8, LANES), jnp.int32),
                vmem((2, levels, LANES), f32),
                dma((2,)),
                dma((5,)),
                dma((3, 2)),
                dma((3, 2)),
                dma((3,)),
                dma((3,)),
                dma((3, 2)),
                dma((3,)),
                dma((3,)),
                dma((3, 2)),
            ],
            compiler_params=pltpu.CompilerParams(
                collective_id=0, has_side_effects=True, vmem_limit_bytes=60 * 1024 * 1024
            ),
        )(fields, metric, jnp.transpose(seam_table, (2, 1, 0)), damp_four, damp_six)
        return jnp.transpose(result, (2, 0, 1, 3))

    placed = (
        P("member", "ty", None, None),
        P("member"),
        P("member"),
        P(None, "ty", None, None),
        P(),
    )
    return jax.shard_map(
        per_device,
        mesh=mesh,
        in_specs=placed,
        out_specs=P("member", "ty", None, None),
        check_vma=False,
    )
```

time: 99.4 us -> 77.1 us (0.78)
  local copies, waits for them, and re-layouts: 16.2 us -> 4.03 us
  Pallas kernels: 82.1 us -> 72.8 us
    pallas_call x1, Pallas kernels: 82.1 us -> 72.8 us  [per_device(): pl.pallas_call(functools.partial(kernel, n), out_shape=jax.ShapeDtypeStru...]
    pallas_call x1 -> x0, local copies, waits for them, and re-layouts: 6.18 us -> none  [per_device(): pl.pallas_call(functools.partial(kernel, n), out_shape=jax.ShapeDtypeStru...]
    unnamed x2 -> x1, local copies, waits for them, and re-layouts: 8.66 us -> 4.03 us
where the time goes in v2:
time: 77.1 us; the launch traced here: 76.9 us
  Pallas kernels  72.8 us (94%)
  local copies, waits for them, and re-layouts  4.03 us (5%)
    pallas_call x1, Pallas kernels, per_device(): pl.pallas_call(functools.partial(kernel, n), out_shape=jax.ShapeDtypeStru...  72.8 us
    unnamed x1, local copies, waits for them, and re-layouts  4.03 us

profile of v2, /device:TPU:38, one launch (start us, length us, event | category | flops | bytes accessed | tf_op | source)
XLA Modules:
  0.0 76.9 jit_solution(6044301625569862616)
XLA Ops:
  0.0 72.8 %shard_map.55 = f32[12,6,16,768]{3,2,1,0:T(8,128)} custom-call(f32[12,6,16,768]{3,2,1,0:T(8,128)} %bitcast.5, f32[12,6,4,768]{3,2,1,0:T(4,128)} %bitcast.6, s32[3,4,6]{2,1,0:T(4,128)} %bitcast.7, f32[16]{0:T(128)} %damp_four.1, f32[16]{0:T(128)} %damp_six.1), custom_call_target="tpu_custom_call" | custom-call | tf_op jit(solution)/shard_map/pallas_call | solution.py:515
  72.9 4.0 %copy.7 = f32[16,12,6,768]{3,0,2,1:T(8,128)} copy(f32[16,12,6,768]{3,0,2,1:T(8,128)} %bitcast.4) | data formatting | bytes 7077888

commit v3 on v2

--- a/solution.py
+++ b/solution.py
@@ -57,9 +57,10 @@
 def kernel(
     n, fields_hbm, metric_hbm, seam, damp_four, damp_six, out_hbm,
     f0, f1, f2, out, met, row_halo, own, mirror, piece_send, piece_all, piece_out, piece_in,
-    stack, turned, turned_part, rim_weight, rest, extract, part, cell_metric, corner_metric,
+    stack, turned, rest, picks, part_pieces, weight_pieces, relayed, extract, part, cell_metric, corner_metric,
     fix, fix_turned, k_halo, k_far, codes, damp,
     load_sem, store_sem, row_send, row_recv, mir_send, mir_recv, far_send, far_recv, fan_send, fan_recv,
+    relay_send, relay_recv,
 ):
     rows, faces, levels, width = f0.shape
     shift = levels.bit_length() - 1
@@ -73,6 +74,19 @@
     above, below = lax.rem(me + 1, n), lax.rem(me + last, n)
     opposite = last - me
 
+    reach, stride = 3 * n // 16, n // 4
+
+    def in_lower(device):
+        return jnp.logical_and(device >= n // 2 - reach, device < n // 2)
+
+    def in_upper(device):
+        return jnp.logical_and(device >= n // 2, device < n // 2 + reach)
+
+    middle_strip = jnp.logical_or(in_lower(me), in_upper(me))
+    helper = jnp.where(in_lower(me), me - stride, me + stride)
+    helps = jnp.logical_or(in_lower(me + stride), in_upper(me - stride))
+    client = jnp.where(in_lower(me + stride), me + stride, me - stride)
+
     load_fields = pltpu.make_async_copy(fields_hbm, f0, load_sem.at[0])
     load_metric = pltpu.make_async_copy(metric_hbm, met, load_sem.at[1])
     load_fields.start()
@@ -90,7 +104,13 @@
     @pl.when(special)
     def _():
         def one(i, _):
-            greet(spread(i))
+            device = spread(i)
+            skipped = jnp.logical_or(in_lower(device), in_upper(device))
+
+            @pl.when(jnp.logical_or(at_first, jnp.logical_not(skipped)))
+            def _():
+                greet(device)
+
             return 0
 
         lax.fori_loop(0, last, one, 0)
@@ -102,6 +122,10 @@
     @pl.when(jnp.logical_not(at_last))
     def _():
         greet(last)
+
+    @pl.when(helps)
+    def _():
+        greet(client)
 
     greet(above)
     greet(below)
@@ -197,6 +221,26 @@
             device_id_type=MESH,
         )
 
+    def to_helper():
+        return pltpu.make_async_remote_copy(
+            src_ref=piece_send.at[0, 1],
+            dst_ref=relayed,
+            send_sem=far_send.at[0, 1],
+            recv_sem=relay_recv,
+            device_id={"ty": helper},
+            device_id_type=MESH,
+        )
+
+    def for_client():
+        return pltpu.make_async_remote_copy(
+            src_ref=relayed,
+            dst_ref=piece_all.at[0, client],
+            send_sem=relay_send,
+            recv_sem=far_recv.at[0],
+            device_id={"ty": last},
+            device_id_type=MESH,
+        )
+
     def fan_copy(round_, device):
         return pltpu.make_async_remote_copy(
             src_ref=piece_out.at[round_, device],
@@ -223,9 +267,18 @@
         def _():
             far_copy(round_, 0).start()
 
-        @pl.when(jnp.logical_not(at_last))
-        def _():
-            far_copy(round_, 1).start()
+        if round_ == 0:
+            @pl.when(middle_strip)
+            def _():
+                to_helper().start()
+
+            @pl.when(jnp.logical_not(jnp.logical_or(middle_strip, at_last)))
+            def _():
+                far_copy(round_, 1).start()
+        else:
+            @pl.when(jnp.logical_not(at_last))
+            def _():
+                far_copy(round_, 1).start()
 
         mirror_copy(round_).start()
 
@@ -251,32 +304,66 @@
             piece_out[round_, j] = jnp.where(flag, there, here)
 
     def send_fan(round_):
+        batch = max(k for k in range(1, 10) if (n - 1) % k == 0)
+
         def one(i, _):
-            fan_copy(round_, spread(i)).start()
+            for k in range(batch):
+                fan_copy(round_, spread(i * batch + k)).start()
             return 0
 
-        lax.fori_loop(0, last, one, 0)
+        lax.fori_loop(0, last // batch, one, 0)
         piece_in[round_, side] = piece_out[round_, me]
 
-    def local_seams(round_):
-        code = codes[pl.ds(side, 1), :]
-        same = level_eye(square, code, 2 * side, shift)
-        other = level_eye(square, code, 2 - 2 * side, shift)
+    def local_seams(round_, source, target, final):
         up = lax.broadcasted_iota(jnp.int32, square, 0)
         across = lax.broadcasted_iota(jnp.int32, square, 1)
         flip = jnp.where(up + across == LANES - 1, 1.0, 0.0).astype(jnp.bfloat16)
-        turn_into(rest, row_halo[round_, side])
-        for b in range(blocks):
+        picks[0] = source[rim_row]
+        picks[1] = row_halo[round_, side]
+        for face in range(faces):
+            joined, edge = seam[0, 2 * side, face], seam[1, 2 * side, face]
+            stack[face] = jnp.where(edge == 2 * side, picks[0, joined], 0.0)
+
+        def flipped(b):
             span = slice(b * LANES, (b + 1) * LANES)
-            back = slice((blocks - 1 - b) * LANES, (blocks - b) * LANES)
-            flipped = exact_left_dot(flip, turned[back, :])
-            rest[span, :] = exact_dot(flipped, same) + exact_dot(rest[span, :], other)
+            return exact_dot(stack[:, :, span].reshape(LANES, LANES), flip).reshape(PAD, levels, LANES)
+
+        for b in range((blocks + 1) // 2):
+            c = blocks - 1 - b
+            one, two = flipped(b), flipped(c)
+            stack[:, :, c * LANES : (c + 1) * LANES] = one
+            stack[:, :, b * LANES : (b + 1) * LANES] = two
+        for face in range(faces):
+            joined, edge = seam[0, 2 * side, face], seam[1, 2 * side, face]
+            value = stack[face] + jnp.where(edge == 2 - 2 * side, picks[1, joined], 0.0)
+            value = met[rim_row, face, pl.ds(2 + side, 1), :] * value
+            if final:
+                value = jnp.concatenate([damp[1]] * blocks, axis=1) * value
+            target[rim_row, face] += value
 
     def join_far(round_):
         flag = codes[pl.ds(2 + side, 1), :] == 1
         for j in range(n):
             span = slice(rows * j, rows * (j + 1))
-            rest[span, :] += jnp.where(flag, piece_all[round_, last - j], piece_all[round_, j])
+            rest[span, :] = jnp.where(flag, piece_all[round_, last - j], piece_all[round_, j])
+
+    def pack_joined(round_):
+        flag = codes[pl.ds(2 + side, 1), :] == 1
+        row = lax.broadcasted_iota(jnp.int32, (rows, LANES), 0)
+        for j in range(n // 2):
+            k = last - j
+            low, high = piece_all[round_, j], piece_all[round_, k]
+            one = part_pieces[j] + weight_pieces[j] * jnp.where(flag, high, low)
+            two = part_pieces[k] + weight_pieces[k] * jnp.where(flag, low, high)
+            if j == 0:
+                one = one + jnp.where(row == 0, fix[pl.ds(rim_row, 1), :], 0.0)
+                two = two + jnp.where(row == rows - 1, fix[pl.ds(16 + rim_row, 1), :], 0.0)
+            piece_out[round_ + 1, j] = jnp.where(flag, two, one)
+            piece_out[round_ + 1, k] = jnp.where(flag, one, two)
+
+    def cut(target, source):
+        for j in range(n):
+            target[j] = source[rows * j : rows * (j + 1), :]
 
     def apply_interior(source, target, final):
         halves = levels // 8
@@ -368,7 +455,8 @@
             stack[face] = jnp.broadcast_to(met[rim_row, face, pl.ds(2 + side, 1), :], (levels, width))
         for b in range(blocks):
             span = slice(b * LANES, (b + 1) * LANES)
-            rim_weight[span, :] = stack[:, :, span].reshape(LANES, LANES).T
+            rest[span, :] = stack[:, :, span].reshape(LANES, LANES).T
+        cut(weight_pieces, rest)
         turn_into(turned, f0[rim_row])
         pack_fan(0)
 
@@ -392,6 +480,11 @@
         apply_interior(source, target, final)
         if final:
             store_copy(0).start()
+        if round_ == 0:
+            @pl.when(helps)
+            def _():
+                to_helper().wait_recv()
+                for_client().start()
 
         row_copy(round_, 0).wait_recv()
         row_copy(round_, 1).wait_recv()
@@ -403,24 +496,27 @@
         @pl.when(jnp.logical_not(at_last))
         def _():
             add_row(target, rows - 1, 3, lambda face: row_halo[round_, 1, face], final)
+
+        @pl.when(special)
+        def _():
+            local_seams(round_, source, target, final)
 
         if not final:
             west, east = take_columns(target)
             part[0] = west
             part[1] = east
 
-        @pl.when(special)
-        def _():
-            local_seams(round_)
-            if not final:
-                turn_into(turned_part, target[rim_row])
-            all_but_one(piece_all.at[round_], far_recv.at[round_]).wait()
-            join_far(round_)
-            if not final:
-                part[0, pl.ds(rim_row, 1), :] += corner_metric[0] * rest[0:1, :]
-                part[1, pl.ds(rim_row, 1), :] += corner_metric[1] * rest[width - 1 : width, :]
+            @pl.when(special)
+            def _():
+                turn_into(turned, target[rim_row])
+                cut(part_pieces, turned)
 
         mirror_copy(round_).wait_recv()
+        near = jnp.concatenate(
+            [own[round_, 0], own[round_, 1], rows_reversed(mirror[round_, 0]), rows_reversed(mirror[round_, 1])],
+            axis=1,
+        )
+        halo = exact_dot(near, k_halo[: 4 * LANES, :])
 
         @pl.when(jnp.logical_not(at_first))
         def _():
@@ -431,50 +527,54 @@
             pltpu.make_async_copy(piece_in.at[round_, 1], piece_in.at[round_, 1], fan_recv.at[round_, 1]).wait()
 
         from_south, from_north = piece_in[round_, 0], piece_in[round_, 1]
-        candidates = jnp.concatenate(
+        far = jnp.concatenate(
             [
-                own[round_, 0],
-                own[round_, 1],
-                rows_reversed(mirror[round_, 0]),
-                rows_reversed(mirror[round_, 1]),
                 jnp.where(reversed_south, rows_reversed(from_south), from_south),
                 jnp.where(reversed_north, rows_reversed(from_north), from_north),
             ],
             axis=1,
         )
-        halo = exact_dot(candidates, k_halo[...])
+        halo = halo + exact_dot(far, k_halo[4 * LANES :, :])
         west = cell_metric[0] * halo[:, :LANES]
         east = cell_metric[1] * halo[:, LANES:]
         fix[0:rows, :] = west
         fix[16 : 16 + rows, :] = east
+
         if not final:
+            @pl.when(special)
+            def _():
+                all_but_one(piece_all.at[round_], far_recv.at[round_]).wait()
+                pack_joined(round_)
+                send_fan(round_ + 1)
+                flag = codes[pl.ds(2 + side, 1), :] == 1
+                low, high = piece_all[round_, 0], piece_all[round_, last]
+                west_end = jnp.where(flag, high, low)[0:1]
+                east_end = jnp.where(flag, low, high)[rows - 1 : rows]
+                part[0, pl.ds(rim_row, 1), :] += corner_metric[0] * west_end
+                part[1, pl.ds(rim_row, 1), :] += corner_metric[1] * east_end
+
             own[round_ + 1, 0] = part[0] + west
             own[round_ + 1, 1] = part[1] + east
             make_far_pieces(round_ + 1)
             send_columns(round_ + 1)
 
-            @pl.when(special)
-            def _():
-                turned[...] = turned_part[...] + rim_weight[...] * rest[...]
-                turned[0:1, :] += fix[pl.ds(rim_row, 1), :]
-                turned[width - 1 : width, :] += fix[pl.ds(16 + rim_row, 1), :]
-                pack_fan(round_ + 1)
-                send_fan(round_ + 1)
+        fix_turned[...] = fix[...].T.reshape(PAD, levels, LANES)
+        if final:
+            add_columns(target, range(rows), True)
 
         @pl.when(special)
         def _():
+            if final:
+                all_but_one(piece_all.at[round_], far_recv.at[round_]).wait()
+            join_far(round_)
             for b in range(blocks):
                 span = slice(b * LANES, (b + 1) * LANES)
                 stack[:, :, span] = rest[span, :].T.reshape(PAD, levels, LANES)
             add_row(target, rim_row, 2 + side, lambda face: stack[face], final)
 
-        fix_turned[...] = fix[...].T.reshape(PAD, levels, LANES)
         if final:
-            store_copy(1).start()
-            store_copy(2).start()
-            add_columns(target, range(rows), True)
-            store_copy(3).start()
-            store_copy(4).start()
+            for index in range(1, 5):
+                store_copy(index).start()
         else:
             add_columns(target, (0, rows - 1), False)
             send_rows(round_ + 1)
@@ -496,6 +596,10 @@
         @pl.when(special)
         def _():
             all_but_one(piece_out.at[round_], fan_send.at[round_]).wait()
+
+    @pl.when(helps)
+    def _():
+        for_client().wait_send()
 
     for index in range(5):
         store_copy(index).wait()
@@ -533,8 +637,10 @@
                 vmem((PAD, levels, width), f32),
                 vmem((width, LANES), f32),
                 vmem((width, LANES), f32),
-                vmem((width, LANES), f32),
-                vmem((width, LANES), f32),
+                vmem((2, faces, levels, width), f32),
+                vmem((n, rows, LANES), f32),
+                vmem((n, rows, LANES), f32),
+                vmem((rows, LANES), f32),
                 vmem((PAD, levels, LANES), f32),
                 vmem((2, rows, LANES), f32),
                 vmem((2, rows, LANES), f32),
@@ -555,6 +661,8 @@
                 dma((3,)),
                 dma((3,)),
                 dma((3, 2)),
+                dma,
+                dma,
             ],
             compiler_params=pltpu.CompilerParams(
                 collective_id=0, has_side_effects=True, vmem_limit_bytes=60 * 1024 * 1024

time: 77.1 us -> 74 us (0.960)
  Pallas kernels: 72.8 us -> 69.8 us
    pallas_call x1, Pallas kernels: 72.8 us -> 69.8 us  [per_device(): pl.pallas_call(functools.partial(kernel, n), out_shape=jax.ShapeDtypeStru...]
where the time goes in v3:
time: 74 us; the launch traced here: 73.8 us
  Pallas kernels  69.8 us (94%)
  local copies, waits for them, and re-layouts  4.03 us (5%)
    pallas_call x1, Pallas kernels, per_device(): pl.pallas_call(functools.partial(kernel, n), out_shape=jax.ShapeDtypeStru...  69.8 us
    unnamed x1, local copies, waits for them, and re-layouts  4.03 us

profile of v3, /device:TPU:38, one launch (start us, length us, event | category | flops | bytes accessed | tf_op | source)
XLA Modules:
  0.0 73.8 jit_solution(1356839579626359006)
XLA Ops:
  0.0 69.8 %shard_map.55 = f32[12,6,16,768]{3,2,1,0:T(8,128)} custom-call(f32[12,6,16,768]{3,2,1,0:T(8,128)} %bitcast.5, f32[12,6,4,768]{3,2,1,0:T(4,128)} %bitcast.6, s32[3,4,6]{2,1,0:T(4,128)} %bitcast.7, f32[16]{0:T(128)} %damp_four.1, f32[16]{0:T(128)} %damp_six.1), custom_call_target="tpu_custom_call" | custom-call | tf_op jit(solution)/shard_map/pallas_call | solution.py:619
  69.8 4.0 %copy.7 = f32[16,12,6,768]{3,0,2,1:T(8,128)} copy(f32[16,12,6,768]{3,0,2,1:T(8,128)} %bitcast.4) | data formatting | bytes 7077888

commit v4 on v3

--- a/solution.py
+++ b/solution.py
@@ -424,9 +424,9 @@
         if index == 0:
             span = (pl.ds(1, rows - 2), slice(None), slice(None), middle)
         elif index < 3:
-            span = ((0, rows - 1)[index - 1], slice(None), slice(None), middle)
+            span = ((0, rows - 1)[index - 1],)
         else:
-            span = (slice(None), slice(None), slice(None), pl.ds((0, width - LANES)[index - 3], LANES))
+            span = (pl.ds(1, rows - 2), slice(None), slice(None), pl.ds((0, width - LANES)[index - 3], LANES))
         return pltpu.make_async_copy(out.at[span], out_hbm.at[span], store_sem.at[index])
 
     load_fields.wait()
@@ -561,6 +561,8 @@
         fix_turned[...] = fix[...].T.reshape(PAD, levels, LANES)
         if final:
             add_columns(target, range(rows), True)
+            store_copy(3).start()
+            store_copy(4).start()
 
         @pl.when(special)
         def _():
@@ -573,8 +575,8 @@
             add_row(target, rim_row, 2 + side, lambda face: stack[face], final)
 
         if final:
-            for index in range(1, 5):
-                store_copy(index).start()
+            store_copy(1).start()
+            store_copy(2).start()
         else:
             add_columns(target, (0, rows - 1), False)
             send_rows(round_ + 1)
@@ -615,11 +617,13 @@
         f32, bf16 = jnp.float32, jnp.bfloat16
         vmem, dma = pltpu.VMEM, pltpu.SemaphoreType.DMA
         any_space = pl.BlockSpec(memory_space=pl.ANY)
+        in_hbm = pl.BlockSpec(memory_space=pltpu.HBM)
         in_smem = pl.BlockSpec(memory_space=pltpu.SMEM)
+        operands = (fields, metric, jnp.transpose(seam_table, (2, 1, 0)), damp_four, damp_six)
         result = pl.pallas_call(
             functools.partial(kernel, n),
             out_shape=jax.ShapeDtypeStruct(fields.shape, f32),
-            in_specs=[any_space, any_space, in_smem, in_smem, in_smem],
+            in_specs=[in_hbm, in_hbm, in_smem, in_smem, in_smem],
             out_specs=any_space,
             scratch_shapes=[
                 vmem(fields.shape, f32),
@@ -665,9 +669,9 @@
                 dma,
             ],
             compiler_params=pltpu.CompilerParams(
-                collective_id=0, has_side_effects=True, vmem_limit_bytes=60 * 1024 * 1024
+                collective_id=0, has_side_effects=True, vmem_limit_bytes=47 * 1024 * 1024
             ),
-        )(fields, metric, jnp.transpose(seam_table, (2, 1, 0)), damp_four, damp_six)
+        )(*(pltpu.with_memory_space_constraint(x, pltpu.HBM) for x in operands))
         return jnp.transpose(result, (2, 0, 1, 3))
 
     placed = (

time: 74 us -> 70.7 us (0.955)
  local copies, waits for them, and re-layouts: 4.03 us -> 1.8 us
  Pallas kernels: 69.8 us -> 68.8 us
    unnamed x1, local copies, waits for them, and re-layouts: 4.03 us -> 1.8 us
    pallas_call x1, Pallas kernels: 69.8 us -> 68.8 us  [per_device(): pl.pallas_call(functools.partial(kernel, n), out_shape=jax.ShapeDtypeStru...]
where the time goes in v4:
time: 70.7 us; the launch traced here: 70.6 us
  Pallas kernels  68.8 us (97%)
  local copies, waits for them, and re-layouts  1.8 us (3%)
    pallas_call x1, Pallas kernels, per_device(): pl.pallas_call(functools.partial(kernel, n), out_shape=jax.ShapeDtypeStru...  68.8 us
    unnamed x1, local copies, waits for them, and re-layouts  1.8 us

profile of v4, /device:TPU:38, one launch (start us, length us, event | category | flops | bytes accessed | tf_op | source)
XLA Modules:
  0.0 70.6 jit_solution(16860162234911142622)
XLA Ops:
  0.0 68.8 %shard_map.55 = f32[12,6,16,768]{3,2,1,0:T(8,128)S(1)} custom-call(f32[12,6,16,768]{3,2,1,0:T(8,128)} %bitcast.5, f32[12,6,4,768]{3,2,1,0:T(4,128)} %bitcast.6, s32[3,4,6]{2,1,0:T(4,128)} %bitcast.7, f32[16]{0:T(128)} %damp_four.1, f32[16]{0:T(128)} %damp_six.1), custom_call_target="tpu_custom_call" | custom-call | tf_op jit(solution)/shard_map/pallas_call | solution.py:623
  68.8 1.8 %copy.7 = f32[16,12,6,768]{3,0,2,1:T(8,128)} copy(f32[16,12,6,768]{3,0,2,1:T(8,128)S(1)} %bitcast.4) | data formatting | bytes 7077888
